TPU v7x, 32 devices: a whole 2x2x4 slice. The times are simulated.
32 devices in a mesh: groups: 2 (over y), seg: 4 (over z), section: 4 (over x, core).
Axes of the slice: x: 2, y: 2, z: 4, core: 2. Of those that a mesh axis runs over, the one named last changes fastest.
Arguments:
- writes: bfloat16 [8, 128, 2048], P(('groups', 'seg'), None, 'section'), parts along dimension 0, may hold values from -6 to 6
- layer_inputs: bfloat16 [4, 8, 256, 2048], P('section', ('groups', 'seg')), parts along dimension 1, may hold values from -6 to 6
- upstream: bfloat16 [4, 8, 256, 2048], P('section', ('groups', 'seg')), parts along dimension 1, may hold values from -6 to 6
- pattern: int32 [8, 2, 3], P(('groups', 'seg')), parts along dimension 0, may hold values 0 or 1
- w_q: bfloat16 [4, 2048, 1024], P('section', 'seg'), may hold values from -0.125 to 0.125
- w_kv: bfloat16 [4, 2048, 512], P('section', 'seg'), may hold values from -0.125 to 0.125
- w_o: bfloat16 [4, 1024, 2048], P('section', 'seg'), may hold values from -0.1875 to 0.1875
- norm_gain: float32 [4, 2048], P('section'), may hold values from 0.5 to 10
- gate_weight: float32 [4, 2048, 16], P('section'), may hold values from -0.125 to 0.125
- gate_bias: float32 [4, 16], P('section'), may hold values from -2 to 6
Outputs:
- section_grads: bfloat16 [4, 8, 256, 2048], P('section', ('groups', 'seg')), parts along dimension 1
- memory_grads: bfloat16 [4, 8, 128, 2048], P('section', ('groups', 'seg')), parts along dimension 1
There are 2 independent parts, one for each index of `groups`. A program takes and returns all parts, laid end to end along the dimension named above; an argument that names none is the same for every part. Nothing has to cross between parts.
All inputs are finite; a program needn't handle non-finite values. No bound on the sum of `pattern` on one device may be relied on, other than what follows from the above.
Results may differ from a plain program's by a relative error of at most 0.03.
The roundings to bfloat16 on the way count: a program that leaves them out, or rounds other values in their place, can miss the bound.
Values may be sent and summed in bfloat16 or wider, within the bound.
A program may use at most 128 MiB of HBM per device.

v0:
```python
import jax
import jax.numpy as jnp
from jax import lax
from jax.sharding import PartitionSpec as P

HEADS = 16
KV_HEADS = 4
HEAD = 64
BLK = 128
MEM = 128


epsilon = 1e-05
masked_score = -1e30


def carried_in(part, axis, combine, identity):
    place = lax.axis_index(axis)
    gathered = jax.tree.map(lambda a: lax.all_gather(a, axis), part)
    state = jax.tree.map(lambda a, e: jnp.zeros_like(a) + jnp.asarray(e, a.dtype), part, identity)

    def one(lap, state):
        return combine(
            state, jax.tree.map(lambda a: lax.dynamic_index_in_dim(a, lap, 0, False), gathered)
        )

    return lax.fori_loop(0, place, one, state)


def normed_rows(values, gain):
    widened = values.astype(jnp.float32)
    scale = lax.rsqrt(jnp.mean(widened * widened, axis=-1, keepdims=True) + epsilon)
    return (widened * scale * gain).astype(jnp.bfloat16)


def allowed_keys(positions, layout, block_rows, memory_rows, total_rows):
    blocks = layout.shape[0]
    query_block = positions // block_rows
    chooser = (query_block[:, None] == jnp.arange(blocks, dtype=jnp.int32)[None, :]).astype(
        jnp.int32
    )
    picked = jnp.sum(chooser[:, :, None] * layout[None, :, :], axis=1)
    token_index = jnp.arange(total_rows, dtype=jnp.int32)
    key_block = token_index // block_rows
    spread = (key_block[None, :] == jnp.arange(blocks, dtype=jnp.int32)[:, None]).astype(jnp.int32)
    token_pattern = jnp.sum(picked[:, 1:, None] * spread[None, :, :], axis=1)
    earlier = (key_block[None, :] < query_block[:, None]) & (token_pattern > 0)
    causal = (key_block[None, :] == query_block[:, None]) & (
        token_index[None, :] <= positions[:, None]
    )
    memory_part = jnp.broadcast_to((picked[:, 0] > 0)[:, None], (positions.shape[0], memory_rows))
    return jnp.concatenate([memory_part, earlier | causal], axis=1)


def attend_rows(queries, keyvals, allowed):
    count = queries.shape[0]
    sources = keyvals.shape[0]
    grouped = queries.reshape(count, KV_HEADS, HEADS // KV_HEADS, HEAD)
    keys = keyvals[:, : KV_HEADS * HEAD].reshape(sources, KV_HEADS, HEAD)
    values = keyvals[:, KV_HEADS * HEAD :].reshape(sources, KV_HEADS, HEAD)
    scores = jnp.einsum(
        "qgre,sge->grqs", grouped, keys, preferred_element_type=jnp.float32
    ) * HEAD ** (-0.5)
    scores = jnp.where(allowed[None, None], scores, masked_score)
    peak = lax.stop_gradient(jnp.max(scores, axis=-1, keepdims=True))
    weights = jnp.exp(scores - peak)
    probs = (weights / jnp.sum(weights, axis=-1, keepdims=True)).astype(jnp.bfloat16)
    mixed = jnp.einsum("grqs,sge->qgre", probs, values, preferred_element_type=jnp.float32)
    return mixed.reshape(count, HEADS * HEAD).astype(jnp.bfloat16)


def apply_layer(stream, memory, layout, query_weight, pair_weight, out_weight, gain):
    memory_rows = memory.shape[0]
    count = stream.shape[0]
    normed = normed_rows(jnp.concatenate([memory, stream], axis=0), gain)
    queries = jnp.dot(
        normed[memory_rows:], query_weight, preferred_element_type=jnp.float32
    ).astype(jnp.bfloat16)
    keyvals = jnp.dot(normed, pair_weight, preferred_element_type=jnp.float32).astype(jnp.bfloat16)
    positions = jnp.arange(count, dtype=jnp.int32)
    allowed = allowed_keys(positions, layout, BLK, memory_rows, count)
    mixed = attend_rows(queries, keyvals, allowed)
    added = jnp.dot(mixed, out_weight, preferred_element_type=jnp.float32)
    return (stream.astype(jnp.float32) + added).astype(jnp.bfloat16)


def per_device(
    writes, layer_inputs, upstream, pattern, w_q, w_kv, w_o, norm_gain, gate_weight, gate_bias
):
    gathered_writes = lax.all_gather(writes, "section", axis=2, tiled=True)
    full_query, full_pair, full_out = (
        lax.all_gather(w_q, "seg", axis=1, tiled=True),
        lax.all_gather(w_kv, "seg", axis=1, tiled=True),
        lax.all_gather(w_o, "seg", axis=1, tiled=True),
    )
    query_weight = full_query[0]
    pair_weight = full_pair[0]
    out_weight = full_out[0]
    rows_in = layer_inputs[0, 0]
    incoming = upstream[0, 0]
    layout = pattern[0]
    gain = norm_gain[0]
    gate_matrix = gate_weight[0]
    gate_offset = gate_bias[0]
    width = rows_in.shape[1]
    widened = gathered_writes[0].astype(jnp.float32)
    logits = jnp.dot(widened, gate_matrix, precision=lax.Precision.HIGHEST) + gate_offset
    keep = jax.nn.sigmoid(logits)
    fresh = ((1.0 - keep)[:, :, None] * widened.reshape(MEM, HEADS, width // HEADS)).reshape(
        MEM, width
    )

    def compose(former, latter):
        carried = latter[0][:, :, None] * former[1].reshape(MEM, HEADS, width // HEADS)
        return (former[0] * latter[0], carried.reshape(MEM, width) + latter[1])

    identity = (jnp.ones_like(keep), jnp.zeros_like(fresh))
    _, state = carried_in((keep, fresh), "seg", compose, identity)
    memory = state.astype(jnp.bfloat16)

    def mapping(first_arg, second_arg):
        return apply_layer(
            first_arg, second_arg, layout, query_weight, pair_weight, out_weight, gain
        )

    _, pull = jax.vjp(mapping, rows_in, memory)
    grad_rows, grad_memory = pull(incoming)
    return (grad_rows[None, None], grad_memory[None, None])


def solution(mesh):
    placed = (
        P(("groups", "seg"), None, "section"),
        P("section", ("groups", "seg"), None, None),
        P("section", ("groups", "seg"), None, None),
        P(("groups", "seg"), None, None),
        P("section", "seg", None),
        P("section", "seg", None),
        P("section", "seg", None),
        P("section", None),
        P("section", None, None),
        P("section", None),
    )
    return jax.shard_map(
        per_device,
        mesh=mesh,
        in_specs=placed,
        out_specs=(
            P("section", ("groups", "seg"), None, None),
            P("section", ("groups", "seg"), None, None),
        ),
        check_vma=False,
    )
```

profile of v0, /device:TPU:24, one launch (start us, length us, event | category | flops | bytes accessed | tf_op | source)
XLA Modules:
  0.0 325.3 jit_solution(520226443879086521)
XLA Ops:
  7.2 0.0 copy-start
  7.2 0.0 all-gather.6.cloned.1.call-start
  7.2 0.7 all-gather.6.cloned.1.call-update
  7.9 0.0 all-gather.8.cloned.1.call-start
  8.0 7.4 %all_gather.22 = bf16[1,128,2048]{2,1,0:T(8,128)(2,1)S(1)} all-gather(bf16[1,128,512]{2,1,0:T(8,128)(2,1)} %param.12), channel_id=1, replica_groups=mesh['groups'=2,'seg'=4,'section'=4] {'section'}, dimensions={2}, use_global_device_ids=true | all-gather | bytes 655360 | tf_op jit(solution)/shard_map/all_gather | solution.py:90
  15.3 1.2 broadcast_subtract_fusion
  16.5 0.1 copy.43
  16.6 0.3 mul.153
  17.0 0.2 mul.154
  17.2 0.0 copy-start.7
  17.2 0.0 copy-start.3
  17.2 1.1 convert_multiply_fusion.6
  18.3 0.0 all-gather.8.cloned.1.call-update
  18.3 0.0 all-gather.12.cloned.1.call-start
  18.3 0.7 all-gather.12.cloned.1.call-update
  19.0 0.0 all-gather.10.cloned.1.call-start
  19.1 0.5 all-gather.10.cloned.1.call-update
  19.6 0.1 copy.41
  19.7 0.1 multiply_reduce_fusion.1
  19.9 0.1 multiply_reduce_fusion
  20.0 0.1 fusion.53
  20.1 0.1 broadcast_in_dim.69
  20.2 0.1 fusion.59
  20.3 0.2 copy.48
  20.5 0.2 copy.42
  20.7 13.2 %all-gather = f32[512,16]{0,1:T(8,128)S(1)} all-gather(f32[128,16]{0,1:T(8,128)S(1)} %get-tuple-element.82), channel_id=2, replica_groups=mesh['groups'=2,'seg'=4,'section'=4] {'seg'}, dimensions={0}, use_global_device_ids=true | all-gather | bytes 40960 | tf_op jit(solution)/shard_map/all_gather | solution.py:19
  33.9 0.1 copy.57
  34.1 55.0 %all-gather.6.cloned.1.call-done = bf16[1,1024,2048]{2,1,0:T(8,128)(2,1)} async-done(((bf16[1,256,2048]{2,1,0:T(8,128)(2,1)}), bf16[1,1024,2048]{2,1,0:T(8,128)(2,1)}) %all-gather.6.cloned.1.call-update) | async-done | bytes 4194320 | tf_op jit(solution)/shard_map/all_gather | solution.py:94
  89.1 3.5 %fusion.29 = bf16[256,1024]{1,0:T(8,128)(2,1)S(1)} fusion(bf16[1,1024,2048]{2,1,0:T(8,128)(2,1)} %all-gather.6.cloned.1.call-done, bf16[1,1,256,2048]{3,2,1,0:T(8,128)(2,1)S(1)} %copy-done.3), kind=kOutput, calls=%fused_computation.44 | convolution fusion | flops 1074003968 | bytes 5767168 | tf_op jit(solution)/shard_map/transpose(jvp())/dot_general | solution.py:83
  92.6 1.0 copy.40
  93.6 77.1 %all-gather.8.cloned.1.call-done = f32[4,128,2048]{2,1,0:T(8,128)} async-done(((f32[1,128,2048]{2,1,0:T(8,128)}), f32[4,128,2048]{2,1,0:T(8,128)}) %all-gather.8.cloned.1.call-update) | async-done | bytes 4194320 | tf_op jit(solution)/shard_map/all_gather | solution.py:19
  170.7 0.1 broadcast_in_dim.71
  170.8 7.5 %while.12 = (s32[]{:T(128)}, f32[128,2048]{1,0:T(8,128)S(1)}, s32[]{:T(128)}, f32[4,128,16]{2,1,0:T(8,128)S(1)}, f32[4,128,2048]{2,1,0:T(8,128)}, /*index=5*/s32[]{:T(128)}, s32[]{:T(128)}, s32[]{:T(128)}) while((s32[]{:T(128)}, f32[128,2048]{1,0:T(8,128)S(1)}, s32[]{:T(128)}, f32[4,128,16]{2,1,0:T(8,128)S(1)}, f32[4,128,2048]{2,1,0:T(8,128)}, ...), condition=%wide.region_3.4_spmd, body=%wide.region_2.3_spmd.sunk | while | flops 524293 | bytes 5267591 | solution.py:27
  170.8 0.3 mul.251
  171.2 2.1 fusion.74
  173.3 0.3 mul.251
  173.7 2.1 fusion.74
  175.9 0.3 mul.251
  176.2 2.1 fusion.74
  178.3 0.1 convert_element_type.93
  178.4 0.4 fusion.17
  178.8 0.2 copy-done.6
  179.0 0.4 fusion.19
  179.5 72.1 %all-gather.12.cloned.1.call-done = bf16[1,2048,1024]{2,1,0:T(8,128)(2,1)} async-done(((bf16[1,512,1024]{2,1,0:T(8,128)(2,1)}), bf16[1,2048,1024]{2,1,0:T(8,128)(2,1)}) %all-gather.12.cloned.1.call-update) | async-done | bytes 4194320 | tf_op jit(solution)/shard_map/all_gather | solution.py:92
  251.6 4.2 %fusion.32 = bf16[256,1024]{1,0:T(8,128)(2,1)} fusion(bf16[1,2048,1024]{2,1,0:T(8,128)(2,1)} %all-gather.12.cloned.1.call-done, bf16[384,2048]{1,0:T(8,128)(2,1)S(1)} %fusion.19), kind=kOutput, calls=%fused_computation.45 | convolution fusion | flops 1074003968 | bytes 5767168 | tf_op jit(solution)/shard_map/jvp()/dot_general | solution.py:76
  255.8 1.2 copy.46
  257.1 41.0 %all-gather.10.cloned.1.call-done = bf16[1,2048,512]{2,1,0:T(8,128)(2,1)} async-done(((bf16[1,512,512]{2,1,0:T(8,128)(2,1)}), bf16[1,2048,512]{2,1,0:T(8,128)(2,1)}) %all-gather.10.cloned.1.call-update) | async-done | bytes 2097168 | tf_op jit(solution)/shard_map/all_gather | solution.py:93
  298.0 3.0 fusion.35
  301.1 0.2 copy.45
  301.3 0.2 copy.49
  301.5 1.1 fusion.8
  302.6 1.3 fusion.15
  303.9 1.8 fusion.40
  305.7 2.5 fusion.7
  308.3 2.6 fusion.5
  310.9 1.1 fusion.39
  311.9 0.7 fusion.61
  312.6 0.4 copy-done.8
  313.1 1.3 fusion.22
  314.4 0.3 copy-done.9
  314.6 1.3 fusion.20
  316.0 0.8 fusion.16
  316.8 0.8 slice_bitcast_fusion
  317.7 1.1 fusion.45
  (27 shorter events, 0.2 us)
Async XLA Ops:
  7.2 8.2 %copy-start = (f32[1,2048,16]{1,2,0:T(8,128)S(1)}, f32[1,2048,16]{1,2,0:T(8,128)}, u32[]{:S(2)}) copy-start(f32[1,2048,16]{1,2,0:T(8,128)} %param.20) | copy-start | bytes 393220
  7.2 81.9 %all-gather.6.cloned.1.call-start = ((), (), s32[]{:S(2)}) async-start(), calls=%async_computation | async-start | bytes 5242880 | tf_op jit(solution)/shard_map/all_gather | solution.py:94
  7.9 162.8 %all-gather.8.cloned.1.call-start = ((), (), s32[]{:S(2)}) async-start(), calls=%async_computation.1 | async-start | bytes 5242880 | tf_op jit(solution)/shard_map/all_gather | solution.py:19
  17.2 2.5 copy-start.7
  17.2 71.9 %copy-start.3 = (bf16[1,1,256,2048]{3,2,1,0:T(8,128)(2,1)S(1)}, bf16[1,1,256,2048]{3,2,1,0:T(8,128)(2,1)}, u32[]{:S(2)}) copy-start(bf16[1,1,256,2048]{3,2,1,0:T(8,128)(2,1)} %param.14) | copy-start | bytes 3145732
  18.3 233.3 %all-gather.12.cloned.1.call-start = ((), (), s32[]{:S(2)}) async-start(), calls=%async_computation.3 | async-start | bytes 5242880 | tf_op jit(solution)/shard_map/all_gather | solution.py:92
  19.0 279.0 %all-gather.10.cloned.1.call-start = ((), (), s32[]{:S(2)}) async-start(), calls=%async_computation.2 | async-start | bytes 2621440 | tf_op jit(solution)/shard_map/all_gather | solution.py:93
  170.8 7.7 %copy-start.1 = (bf16[1,1,256,2048]{3,2,1,0:T(8,128)(2,1)S(1)}, bf16[1,1,256,2048]{3,2,1,0:T(8,128)(2,1)}, u32[]{:S(2)}) copy-start(bf16[1,1,256,2048]{3,2,1,0:T(8,128)(2,1)} %param.13) | copy-start | bytes 3145732
  178.3 0.7 copy-start.6
  179.5 72.1 %copy-start.2 = (bf16[384,2048]{1,0:T(8,128)(2,1)}, bf16[384,2048]{1,0:T(8,128)(2,1)S(1)}, u32[]{:S(2)}) copy-start(bf16[384,2048]{1,0:T(8,128)(2,1)S(1)} %fusion.19) | copy-start | bytes 4718596
  302.5 1.3 copy-start.5
  310.9 2.2 copy-start.8
  313.1 1.6 copy-start.9
  316.0 1.7 copy-start.4
Sparse Core Ops, SparseCore 0:
  9.6 79.4 all-gather.5
  91.2 79.3 all-gather.7
  172.2 79.2 all-gather.11
  253.0 44.9 all-gather.9
where the time goes:
time: 330 us; the launch traced here: 325 us
  waiting for transfers between devices  247 us (75%)
  matrix products  21.7 us (7%)
  blocking collectives  20.6 us (6%)
  other arithmetic  14.6 us (4%)
  between operations  14.1 us (4%)
  local copies, waits for them, and re-layouts  6.93 us (2%)
    all_gather x1, waiting for transfers between devices, carried_in(): gathered = jax.tree.map(lambda a: lax.all_gather(a, axis), part)  77.1 us
    all_gather x1, waiting for transfers between devices, per_device(): lax.all_gather(w_q, 'seg', axis=1, tiled=True)  72.1 us
    all_gather x1, waiting for transfers between devices, per_device(): lax.all_gather(w_o, 'seg', axis=1, tiled=True)  55 us
    all_gather x1, waiting for transfers between devices, per_device(): lax.all_gather(w_kv, 'seg', axis=1, tiled=True)  41 us
    all_gather x1, blocking collectives, carried_in(): gathered = jax.tree.map(lambda a: lax.all_gather(a, axis), part)  13.2 us
    all_gather x1, blocking collectives, per_device(): gathered_writes = lax.all_gather(writes, 'section', axis=2, tiled=True)  7.38 us
  transfers between devices with their start and end apart: 4, of which 4 were waited for; matrix products, arithmetic and copies ran while one was open for 7% of the time, Pallas kernels for 0%

commit v1 on v0

--- a/solution.py
+++ b/solution.py
@@ -1,6 +1,10 @@
+import functools
+
 import jax
 import jax.numpy as jnp
 from jax import lax
+from jax.experimental import pallas as pl
+from jax.experimental.pallas import tpu as pltpu
 from jax.sharding import PartitionSpec as P
 
 HEADS = 16
@@ -14,17 +18,220 @@
 masked_score = -1e30
 
 
-def carried_in(part, axis, combine, identity):
-    place = lax.axis_index(axis)
-    gathered = jax.tree.map(lambda a: lax.all_gather(a, axis), part)
-    state = jax.tree.map(lambda a, e: jnp.zeros_like(a) + jnp.asarray(e, a.dtype), part, identity)
-
-    def one(lap, state):
-        return combine(
-            state, jax.tree.map(lambda a: lax.dynamic_index_in_dim(a, lap, 0, False), gathered)
-        )
-
-    return lax.fori_loop(0, place, one, state)
+def gather_kernel(
+    n, groups, sections, writes, w_kv, w_q, w_o, all_writes, all_kv, all_q, all_o, *sems
+):
+    up_sem, down_sem, zrecv, ysend, yrecv, wsend, wrecv, psend, precv, local = sems
+    g = lax.axis_index("groups")
+    s = lax.axis_index("seg")
+    c = lax.axis_index("section")
+    weights = ((w_kv, all_kv), (w_q, all_q), (w_o, all_o))
+    wide = writes.shape[1]
+    mine = pl.ds(pl.multiple_of(c * wide, wide), wide)
+
+    barrier = pltpu.get_barrier_semaphore()
+
+    def greet(where):
+        pl.semaphore_signal(
+            barrier, inc=1, device_id=where, device_id_type=pl.DeviceIdType.MESH
+        )
+
+    @pl.when(s > 0)
+    def _():
+        greet((g, s - 1, c))
+
+    @pl.when(s < n - 1)
+    def _():
+        greet((g, s + 1, c))
+
+    for d in range(1, groups):
+        greet(((g + d) % groups, s, c))
+    for d in range(1, sections):
+        greet((g, s, (c + d) % sections))
+
+    beside = (s + n - 1) // n + (2 * n - 2 - s) // n
+    pl.semaphore_wait(barrier, beside + groups + sections - 2)
+
+    def remote(src, dst, send, recv, where):
+        return pltpu.make_async_remote_copy(
+            src_ref=src,
+            dst_ref=dst,
+            send_sem=send,
+            recv_sem=recv,
+            device_id=where,
+            device_id_type=pl.DeviceIdType.MESH,
+        )
+
+    def up(i, shard, own=False):
+        src, dst = weights[i]
+        spot = dst.at[shard, g]
+        return remote(
+            src.at[g] if own else spot, spot, up_sem.at[i, shard], zrecv.at[i, shard], (g, s + 1, c)
+        )
+
+    def down(i, shard, own=False):
+        src, dst = weights[i]
+        spot = dst.at[shard, g]
+        return remote(
+            src.at[g] if own else spot, spot, down_sem.at[i, shard], zrecv.at[i, shard], (g, s - 1, c)
+        )
+
+    def across(i, shard, d):
+        spot = weights[i][1].at[shard, g]
+        return remote(
+            spot, spot, ysend.at[i, shard, d], yrecv.at[i, shard, d], ((g + d) % groups, s, c)
+        )
+
+    def across_in(i, shard, d):
+        spot = weights[i][1].at[shard, (g + groups - d) % groups]
+        return remote(
+            spot, spot, ysend.at[i, shard, d], yrecv.at[i, shard, d], ((g + d) % groups, s, c)
+        )
+
+    def write_up(shard, own=False):
+        spot = all_writes.at[shard, :, mine]
+        return remote(
+            writes if own else spot, spot, wsend.at[shard], wrecv.at[shard], (g, s + 1, c)
+        )
+
+    def write_peer(shard, d):
+        spot = all_writes.at[shard, :, mine]
+        return remote(
+            spot, spot, psend.at[shard, d], precv.at[shard, d], (g, s, (c + d) % sections)
+        )
+
+    def write_peer_in(shard, d):
+        origin = (c + sections - d) % sections
+        spot = all_writes.at[shard, :, pl.ds(pl.multiple_of(origin * wide, wide), wide)]
+        return remote(
+            spot, spot, psend.at[shard, d], precv.at[shard, d], (g, s, (c + d) % sections)
+        )
+
+    def own_copy(i):
+        src, dst = weights[i]
+        return pltpu.make_async_copy(src, dst.at[s], local.at[i])
+
+    def start_own(i):
+        @pl.when(s < n - 1)
+        def _():
+            up(i, s, True).start()
+
+        @pl.when(s > 0)
+        def _():
+            down(i, s, True).start()
+
+        own_copy(i).start()
+
+    @pl.when(s < n - 1)
+    def _():
+        write_up(s, True).start()
+
+    start_own(0)
+
+    @pl.loop(1, n)
+    def _(k):
+        @pl.when(s - k >= 0)
+        def _():
+            write_up(s - k).wait_recv()
+
+            @pl.when(s < n - 1)
+            def _():
+                write_up(s - k).start()
+
+            for d in range(1, sections):
+                write_peer(s - k, d).start()
+
+    for i in range(len(weights)):
+        if i + 1 < len(weights):
+            start_own(i + 1)
+
+        @pl.loop(1, n)
+        def _(k, i=i):
+            @pl.when(s - k >= 0)
+            def _():
+                up(i, s - k).wait_recv()
+
+                @pl.when(s < n - 1)
+                def _():
+                    up(i, s - k).start()
+
+                for d in range(1, groups):
+                    across(i, s - k, d).start()
+
+            @pl.when(s + k < n)
+            def _():
+                down(i, s + k).wait_recv()
+
+                @pl.when(s > 0)
+                def _():
+                    down(i, s + k).start()
+
+                for d in range(1, groups):
+                    across(i, s + k, d).start()
+
+    @pl.loop(0, n)
+    def _(shard):
+        @pl.when(shard < s)
+        def _():
+            for d in range(1, sections):
+                write_peer_in(shard, d).wait_recv()
+                write_peer(shard, d).wait_send()
+
+        @pl.when((shard <= s) & (s < n - 1))
+        def _():
+            write_up(shard).wait_send()
+
+    for i in range(len(weights)):
+
+        @pl.loop(0, n)
+        def _(shard, i=i):
+            @pl.when(shard != s)
+            def _():
+                for d in range(1, groups):
+                    across_in(i, shard, d).wait_recv()
+                    across(i, shard, d).wait_send()
+
+            @pl.when((shard <= s) & (s < n - 1))
+            def _():
+                up(i, shard).wait_send()
+
+            @pl.when((shard >= s) & (s > 0))
+            def _():
+                down(i, shard).wait_send()
+
+        own_copy(i).wait()
+
+
+def gather_all(n, groups, sections, writes, w_kv, w_q, w_o):
+    def halves(w):
+        return w.reshape(groups, w.shape[0] // groups, w.shape[1])
+
+    shards = [halves(w) for w in (w_kv, w_q, w_o)]
+    rows, wide = writes.shape
+    anywhere = pl.BlockSpec(memory_space=pl.ANY)
+    dma = pltpu.SemaphoreType.DMA
+    outs = pl.pallas_call(
+        functools.partial(gather_kernel, n, groups, sections),
+        out_shape=[jax.ShapeDtypeStruct((n, rows, wide * sections), writes.dtype)]
+        + [jax.ShapeDtypeStruct((n, *w.shape), w.dtype) for w in shards],
+        in_specs=[anywhere] * 4,
+        out_specs=[anywhere] * 4,
+        scratch_shapes=[
+            dma((3, n)),
+            dma((3, n)),
+            dma((3, n)),
+            dma((3, n, groups)),
+            dma((3, n, groups)),
+            dma((n,)),
+            dma((n,)),
+            dma((n, sections)),
+            dma((n, sections)),
+            dma((3,)),
+        ],
+        compiler_params=pltpu.CompilerParams(collective_id=0, has_side_effects=True),
+    )(writes, *shards)
+    full = [w.reshape(-1, w.shape[-1]) for w in outs[1:]]
+    return outs[0], *full
 
 
 def normed_rows(values, gain):
@@ -85,38 +292,48 @@
 
 
 def per_device(
-    writes, layer_inputs, upstream, pattern, w_q, w_kv, w_o, norm_gain, gate_weight, gate_bias
+    n,
+    groups,
+    sections,
+    writes,
+    layer_inputs,
+    upstream,
+    pattern,
+    w_q,
+    w_kv,
+    w_o,
+    norm_gain,
+    gate_weight,
+    gate_bias,
 ):
-    gathered_writes = lax.all_gather(writes, "section", axis=2, tiled=True)
-    full_query, full_pair, full_out = (
-        lax.all_gather(w_q, "seg", axis=1, tiled=True),
-        lax.all_gather(w_kv, "seg", axis=1, tiled=True),
-        lax.all_gather(w_o, "seg", axis=1, tiled=True),
-    )
-    query_weight = full_query[0]
-    pair_weight = full_pair[0]
-    out_weight = full_out[0]
+    all_writes, pair_weight, query_weight, out_weight = gather_all(
+        n, groups, sections, writes[0], w_kv[0], w_q[0], w_o[0]
+    )
     rows_in = layer_inputs[0, 0]
     incoming = upstream[0, 0]
     layout = pattern[0]
     gain = norm_gain[0]
-    gate_matrix = gate_weight[0]
-    gate_offset = gate_bias[0]
     width = rows_in.shape[1]
-    widened = gathered_writes[0].astype(jnp.float32)
-    logits = jnp.dot(widened, gate_matrix, precision=lax.Precision.HIGHEST) + gate_offset
-    keep = jax.nn.sigmoid(logits)
-    fresh = ((1.0 - keep)[:, :, None] * widened.reshape(MEM, HEADS, width // HEADS)).reshape(
-        MEM, width
-    )
-
-    def compose(former, latter):
-        carried = latter[0][:, :, None] * former[1].reshape(MEM, HEADS, width // HEADS)
-        return (former[0] * latter[0], carried.reshape(MEM, width) + latter[1])
-
-    identity = (jnp.ones_like(keep), jnp.zeros_like(fresh))
-    _, state = carried_in((keep, fresh), "seg", compose, identity)
-    memory = state.astype(jnp.bfloat16)
+    place = lax.axis_index("seg")
+    earlier = jnp.arange(n) < place
+    widened = jnp.where(earlier[:, None, None], all_writes, 0).astype(jnp.float32)
+    logits = (
+        jnp.dot(
+            widened.reshape(n * MEM, width), gate_weight[0], precision=lax.Precision.HIGHEST
+        )
+        + gate_bias[0]
+    )
+    keep = jax.nn.sigmoid(logits).reshape(n, MEM, HEADS)
+
+    def advance(at, state):
+        share = keep[at][:, :, None]
+        fresh = widened[at].reshape(MEM, HEADS, width // HEADS)
+        return jnp.where(at < place, share * state + (1.0 - share) * fresh, state)
+
+    state = lax.fori_loop(
+        0, n, advance, jnp.zeros((MEM, HEADS, width // HEADS), jnp.float32), unroll=n <= 8
+    )
+    memory = state.reshape(MEM, width).astype(jnp.bfloat16)
 
     def mapping(first_arg, second_arg):
         return apply_layer(
@@ -141,8 +358,9 @@
         P("section", None, None),
         P("section", None),
     )
+    sizes = (mesh.shape["seg"], mesh.shape["groups"], mesh.shape["section"])
     return jax.shard_map(
-        per_device,
+        functools.partial(per_device, *sizes),
         mesh=mesh,
         in_specs=placed,
         out_specs=(

time: 330 us -> 173 us (0.52); the launches traced: 325 us -> 172 us
  waiting for transfers between devices: 247 us -> 0 us
  Pallas kernels: 0 us -> 122 us
  blocking collectives: 20.6 us -> 0 us
  between operations: 14.1 us -> 0.96 us
  local copies, waits for them, and re-layouts: 6.93 us -> 15.1 us
    all_gather x4 -> x0, waiting for transfers between devices: 245 us -> none  [the longest x1 77.1 us: carried_in(): gathered = jax.tree.map(lambda a: lax.all_gather(a, axis), part)]
    pallas_call x0 -> x1, Pallas kernels: none -> 122 us  [gather_all(): pl.pallas_call(functools.partial(gather_kernel, n, groups, sections), out...]
    all_gather x2 -> x0, blocking collectives: 20.6 us -> none  [the longest x1 13.2 us: carried_in(): gathered = jax.tree.map(lambda a: lax.all_gather(a, axis), part)]
    convert_element_type x1 -> x2, other arithmetic: 0.06 us -> 6.88 us  [the longest x1 4.43 us: per_device(): memory = state.reshape(MEM, width).astype(jnp.bfloat16)]
    add x3 -> x0, other arithmetic: 6.42 us -> none  [compose(): return (former[0] * latter[0], carried.reshape(MEM, width) + latter[1])]
  transfers between devices with their start and end apart: 4 -> 0, of which waited for: 4 -> 0; matrix products, arithmetic and copies ran while one was open for 7% -> 0% of each run, Pallas kernels for 0% -> 0%
where the time goes in v1:
time: 173 us; the launch traced here: 172 us
  Pallas kernels  122 us (71%)
  matrix products  20.7 us (12%)
  local copies, waits for them, and re-layouts  15.1 us (9%)
  other arithmetic  14 us (8%)
    pallas_call x1, Pallas kernels, gather_all(): pl.pallas_call(functools.partial(gather_kernel, n, groups, sections), out...  122 us
    convert_element_type x1, other arithmetic, per_device(): memory = state.reshape(MEM, width).astype(jnp.bfloat16)  4.43 us
    dot_general x1, matrix products, apply_layer(): added = jnp.dot(mixed, out_weight, preferred_element_type=jnp.float32)  4.42 us
    dot_general x2, matrix products, attend_rows(): jnp.einsum('grqs,sge->qgre', probs, values, preferred_element_type=jnp.fl...  4.16 us
    dot_general x3, matrix products, attend_rows(): jnp.einsum('qgre,sge->grqs', grouped, keys, preferred_element_type=jnp.fl...  3.76 us
    dot_general x2, matrix products, apply_layer(): jnp.dot(normed[memory_rows:], query_weight, preferred_element_type=jnp.fl...  3.55 us

profile of v1, /device:TPU:24, one launch (start us, length us, event | category | flops | bytes accessed | tf_op | source)
XLA Modules:
  0.0 172.5 jit_solution(9941872124805492615)
XLA Ops:
  0.6 0.0 copy-start
  0.6 0.0 copy-start.4
  0.7 0.9 copy.41
  1.6 0.1 multiply_reduce_fusion.1
  1.7 0.1 broadcast_in_dim.81
  1.8 0.1 multiply_reduce_fusion
  1.9 0.1 fusion.39
  2.1 0.1 fusion.45
  2.1 0.8 copy.54
  2.9 0.8 copy.42
  3.8 121.7 %shard_map.113 = (bf16[4,128,2048]{2,1,0:T(8,128)(2,1)}, bf16[4,2,256,512]{3,2,1,0:T(8,128)(2,1)}, bf16[4,2,256,1024]{3,2,1,0:T(8,128)(2,1)}, bf16[4,2,128,2048]{3,2,1,0:T(8,128)(2,1)}) custom-call(bf16[128,512]{1,0:T(8,128)(2,1)} %bitcast.223, bf16[2,256,512]{2,1,0:T(8,128)(2,1)} %bitcast.217, bf16[2,256,1024]{2,1,0:T(8,128)(2,1)} %bitcast.215, ...), custom_call_target="tpu_custom_call" | custom-call | tf_op jit(solution)/shard_map/pallas_call | solution.py:213
  125.5 0.0 copy-done.4
  125.5 0.0 copy-start.3
  125.5 4.4 %convolution_convert_fusion.5 = bf16[1024,256]{1,0:T(8,128)(2,1)} fusion(bf16[1024,2048]{1,0:T(8,128)(2,1)} %bitcast.231, bf16[1,1,256,2048]{3,2,1,0:T(8,128)(2,1)S(1)} %copy-done.4), kind=kOutput, calls=%fused_computation.34 | convolution fusion | flops 1074003968 | bytes 5767168 | tf_op jit(solution)/shard_map/transpose(jvp())/dot_general | solution.py:290
  129.9 0.0 copy-done.3
  129.9 2.4 %fusion.46 = (f32[4,128,2048]{2,1,0:T(8,128)}, bf16[4,128,2048]{2,1,0:T(8,128)(2,1)S(1)}) fusion(bf16[4,128,2048]{2,1,0:T(8,128)(2,1)S(1)} %copy-done.3, pred[4]{0:T(512)(128)(4,1)S(1)} %iota_compare_fusion.1), kind=kLoop, calls=%fused_computation.102 | loop fusion | flops 2097152 | bytes 8388612 | tf_op jit(solution)/shard_map/convert_element_type | solution.py:319
  132.4 0.0 copy-done
  132.4 0.0 copy-done.9
  132.4 1.7 %fusion.22 = f32[512,16]{0,1:T(8,128)S(1)} fusion(bf16[512,2048]{1,0:T(8,128)(2,1)S(1)} %bitcast.202, f32[1,2048,16]{1,2,0:T(8,128)S(1)} %copy-done, f32[16]{0:T(128)S(1)} %bitcast.228), kind=kOutput, calls=%fused_computation.44 | convolution fusion | flops 201359360 | bytes 2261056 | tf_op jit(solution)/shard_map/dot_general | solution.py:321
  134.2 0.1 copy.43
  134.3 0.1 copy.50
  134.4 0.1 copy.49
  134.5 0.1 copy.48
  134.6 0.1 copy.47
  134.7 0.1 copy.46
  134.8 0.1 copy.45
  134.9 0.1 copy.44
  135.0 0.3 mul.214
  135.3 0.3 mul.216
  135.7 0.3 mul.219
  136.0 0.3 mul.221
  136.3 0.3 mul.225
  136.7 0.3 mul.229
  137.0 0.3 mul.233
  137.3 0.3 mul.212
  137.7 0.2 copy-done.1
  137.8 4.4 %fusion.25 = bf16[128,2048]{1,0:T(8,128)(2,1)S(1)} fusion(f32[16,8,16,128]{3,2,1,0:T(8,128)S(1)} %bitcast.211, f32[16,8,16,128]{3,2,1,0:T(8,128)S(1)} %bitcast.210, f32[16,8,16,128]{3,2,1,0:T(8,128)S(1)} %bitcast.209, f32[16,8,16,128]{3,2,1,0:T(8,128)S(1)} %bitcast.208, f32[16,8,16,128]{3,2,1,0:T(8,128)S(1)} %bitcast.207, ...), kind=kLoop, calls=%fused_computation.48 | loop fusion | flops 4194304 | bytes 13107204 | tf_op jit(solution)/shard_map/convert_element_type | solution.py:336
  142.3 0.4 fusion.10
  142.7 0.4 fusion.12
  143.1 0.7 copy-done.12
  143.9 1.7 %convolution_convert_fusion.6 = bf16[384,512]{1,0:T(8,128)(2,1)} fusion(bf16[384,2048]{1,0:T(8,128)(2,1)S(1)} %fusion.12, bf16[2048,512]{1,0:T(8,128)(2,1)S(1)} %bitcast.232), kind=kOutput, calls=%fused_computation.35 | convolution fusion | flops 805502976 | bytes 4063232 | tf_op jit(solution)/shard_map/jvp()/dot_general | solution.py:286
  145.6 0.6 copy-done.10
  146.2 2.2 %convolution_convert_fusion.4 = bf16[256,1024]{1,0:T(8,128)(2,1)} fusion(bf16[2048,1024]{1,0:T(8,128)(2,1)S(1)} %bitcast.229, bf16[384,2048]{1,0:T(8,128)(2,1)S(1)} %fusion.12), kind=kOutput, calls=%fused_computation.33 | convolution fusion | flops 1074003968 | bytes 5767168 | tf_op jit(solution)/shard_map/jvp()/dot_general | solution.py:283
  148.5 1.2 copy.52
  149.7 1.8 %fusion.47 = (bf16[384,256]{1,0:T(8,128)(2,1)}, bf16[384,256]{1,0:T(8,128)(2,1)}) fusion(bf16[384,512]{1,0:T(8,128)(2,1)} %convolution_convert_fusion.6), kind=kLoop, calls=%fused_computation.103 | loop fusion | bytes 786432 | tf_op jit(solution)/shard_map/jvp()/slice | solution.py:266
  151.5 1.1 copy.51
  152.6 1.7 %copy.55 = bf16[384,256]{0,1:T(8,128)(2,1)} copy(bf16[384,256]{1,0:T(8,128)(2,1)} %get-tuple-element.13) | data formatting | bytes 393216 | tf_op jit(solution)/shard_map/jvp()/slice | solution.py:267
  154.3 2.0 %fusion.7 = (f32[4,4,256]{2,1,0:T(4,128)S(1)}, f32[4,384,256,4]{2,1,3,0:T(8,128)S(1)}) fusion(pred[256,384]{0,1:T(8,128)(4,1)} %copy.42, bf16[384,4,64,1]{0,2,3,1:T(8,128)(2,1)S(1)} %bitcast.213, bf16[256,4,4,64]{0,3,2,1:T(8,128)(2,1)S(1)} %bitcast.203), kind=kOutput, calls=%fused_computation.12 | convolution fusion | flops 206041088 | bytes 7127040 | tf_op jit(solution)/shard_map/jvp(qgre,sge->grqs)/dot_general | solution.py:268
  156.4 0.0 copy-done.5
  156.4 0.0 copy-start.14
  156.4 1.3 fusion.8
  157.7 0.0 copy-start.7
  157.7 1.8 %fusion.18 = bf16[4,64,384]{2,1,0:T(8,128)(2,1)S(1)} fusion(bf16[4,64,4,256]{3,1,2,0:T(8,128)(2,1)S(1)} %bitcast.234, f32[4,384,256,4]{2,1,3,0:T(8,128)S(1)} %get-tuple-element.25, f32[4,4,256]{2,1,0:T(4,128)S(1)} %fusion.8, f32[4,4,256]{2,1,0:T(4,128)S(1)} %get-tuple-element.24, pred[256,384]{0,1:T(8,128)(4,1)S(1)} %copy-done.5), kind=kOutput, calls=%fused_computation.39 | convolution fusion | flops 209289216 | bytes 7143424 | tf_op jit(solution)/shard_map/transpose(jvp(grqs,sge->qgre))/dot_general | solution.py:275
  159.6 2.4 %fusion.6 = (f32[4,4,256]{2,1,0:T(4,128)S(1)}, bf16[4,4,256,384]{2,3,1,0:T(8,128)(2,1)S(1)}) fusion(f32[4,384,256,4]{2,1,3,0:T(8,128)S(1)} %get-tuple-element.25, f32[4,4,256]{2,1,0:T(4,128)S(1)} %multiply_divide_fusion, f32[4,4,256]{2,1,0:T(4,128)S(1)} %get-tuple-element.24, pred[256,384]{0,1:T(8,128)(4,1)S(1)} %copy-done.5, ...), kind=kOutput, calls=%fused_computation.8 | convolution fusion | flops 213905408 | bytes 10305536 | tf_op jit(solution)/shard_map/transpose(jvp(grqs,sge->qgre))/dot_general | solution.py:275
  162.0 2.6 %fusion.4 = bf16[4,384,256,4]{2,1,3,0:T(8,128)(2,1)S(1)} fusion(bf16[4,4,256,384]{2,3,1,0:T(8,128)(2,1)S(1)} %get-tuple-element.27, f32[4,384,256,4]{2,1,3,0:T(8,128)S(1)} %get-tuple-element.25, f32[4,256,4]{1,2,0:T(4,128)S(1)} %bitcast.221, f32[4,256,4]{1,2,0:T(4,128)S(1)} %negate_bitcast_fusion, f32[4,256,4]{1,2,0:T(4,128)S(1)} %bitcast.222, ...), kind=kLoop, calls=%fused_computation.6 | loop fusion | flops 15728640 | bytes 12730368 | tf_op jit(solution)/shard_map/transpose(jvp())/mul | solution.py:268
  164.6 1.1 fusion.17
  165.6 0.7 fusion.49
  166.3 0.4 copy-done.11
  166.7 1.3 convolution_convert_fusion.1
  168.1 0.3 copy-done.13
  168.3 1.4 fusion.13
  169.7 0.8 fusion.9
  170.5 0.8 slice_bitcast_fusion.4
  171.4 1.1 fusion.32
  (26 shorter events, 0.1 us)
Async XLA Ops:
  0.6 131.8 %copy-start = (f32[1,2048,16]{1,2,0:T(8,128)S(1)}, f32[1,2048,16]{1,2,0:T(8,128)}, u32[]{:S(2)}) copy-start(f32[1,2048,16]{1,2,0:T(8,128)} %param.18) | copy-start | bytes 393220
  0.6 124.9 %copy-start.4 = (bf16[1,1,256,2048]{3,2,1,0:T(8,128)(2,1)S(1)}, bf16[1,1,256,2048]{3,2,1,0:T(8,128)(2,1)}, u32[]{:S(2)}) copy-start(bf16[1,1,256,2048]{3,2,1,0:T(8,128)(2,1)} %param.12) | copy-start | bytes 3145732
  125.5 4.4 %copy-start.3 = (bf16[4,128,2048]{2,1,0:T(8,128)(2,1)S(1)}, bf16[4,128,2048]{2,1,0:T(8,128)(2,1)}, u32[]{:S(2)}) copy-start(bf16[4,128,2048]{2,1,0:T(8,128)(2,1)} %get-tuple-element.7) | copy-start | bytes 6291460
  129.9 2.5 %copy-start.9 = (f32[1,16]{1,0:T(1,128)S(1)}, f32[1,16]{1,0:T(1,128)}, u32[]{:S(2)}) copy-start(f32[1,16]{1,0:T(1,128)} %param.19) | copy-start | bytes 196
  135.7 2.2 %copy-start.1 = (f32[4,128,2048]{2,1,0:T(8,128)S(1)}, f32[4,128,2048]{2,1,0:T(8,128)}, u32[]{:S(2)}) copy-start(f32[4,128,2048]{2,1,0:T(8,128)} %get-tuple-element.10) | copy-start | bytes 12582916
  137.8 4.4 %copy-start.2 = (bf16[1,1,256,2048]{3,2,1,0:T(8,128)(2,1)S(1)}, bf16[1,1,256,2048]{3,2,1,0:T(8,128)(2,1)}, u32[]{:S(2)}) copy-start(bf16[1,1,256,2048]{3,2,1,0:T(8,128)(2,1)} %param.11) | copy-start | bytes 3145732
  137.8 4.9 %copy-start.8 = (f32[1,2048]{1,0:T(1,128)S(1)}, f32[1,2048]{1,0:T(1,128)}, u32[]{:S(2)}) copy-start(f32[1,2048]{1,0:T(1,128)} %param.17) | copy-start | bytes 24580
  142.3 1.6 copy-start.12
  143.9 2.3 %copy-start.10 = (bf16[4,2,256,1024]{3,2,1,0:T(8,128)(2,1)S(1)}, bf16[4,2,256,1024]{3,2,1,0:T(8,128)(2,1)}, u32[]{:S(2)}) copy-start(bf16[4,2,256,1024]{3,2,1,0:T(8,128)(2,1)} %get-tuple-element.9) | copy-start | bytes 12582916
  154.3 2.1 %copy-start.5 = (pred[256,384]{0,1:T(8,128)(4,1)S(1)}, pred[256,384]{0,1:T(8,128)(4,1)}, u32[]{:S(2)}) copy-start(pred[256,384]{0,1:T(8,128)(4,1)} %copy.42) | copy-start | bytes 294916
  156.4 1.3 copy-start.14
  157.7 1.8 %copy-start.7 = (bf16[384,256]{0,1:T(8,128)(2,1)S(1)}, bf16[384,256]{0,1:T(8,128)(2,1)}, u32[]{:S(2)}) copy-start(bf16[384,256]{0,1:T(8,128)(2,1)} %copy.55) | copy-start | bytes 589828
  159.6 2.4 %copy-start.6 = (pred[384,256]{1,0:T(8,128)(4,1)S(1)}, pred[384,256]{1,0:T(8,128)(4,1)}, u32[]{:S(2)}) copy-start(pred[384,256]{1,0:T(8,128)(4,1)} %copy.54) | copy-start | bytes 294916
  164.6 2.2 %copy-start.11 = (bf16[4,2,256,1024]{3,2,1,0:T(8,128)(2,1)S(1)}, bf16[4,2,256,1024]{3,2,1,0:T(8,128)(2,1)}, u32[]{:S(2)}) copy-start(bf16[4,2,256,1024]{3,2,1,0:T(8,128)(2,1)} %get-tuple-element.9) | copy-start | bytes 12582916
  166.7 1.6 copy-start.13

commit v2 on v0

v2 whole, which is shorter than its diff:
```python
import functools

import jax
import jax.numpy as jnp
from jax import lax
from jax.experimental import pallas as pl
from jax.experimental.pallas import tpu as pltpu
from jax.sharding import PartitionSpec as P

HEADS = 16
KV_HEADS = 4
HEAD = 64
BLK = 128
MEM = 128


epsilon = 1e-05
masked_score = -1e30
GROUP = HEADS // KV_HEADS
NT = (((1,), (1,)), ((), ()))
TN = (((0,), (0,)), ((), ()))
CHUNKS = KV_HEADS


def layer_kernel(
    n,
    groups,
    sections,
    pattern,
    writes,
    rows_in,
    upstream,
    gain,
    gate,
    gate_bias,
    w_kv,
    w_q,
    w_o,
    grad_rows,
    grad_memory,
    all_writes,
    all_kv,
    all_q,
    all_o,
    normed,
    scales,
    memory,
    state,
    gates,
    keys,
    values,
    bias,
    dmixed,
    dq,
    dkeys,
    dvalues,
    dnormed,
    *sems,
):
    up_sem, down_sem, zrecv, ysend, yrecv, wsend, wrecv, psend, precv, local = sems
    g = lax.axis_index("groups")
    s = lax.axis_index("seg")
    c = lax.axis_index("section")
    count, width = rows_in.shape
    wide = writes.shape[1]
    span = all_q.shape[1] // CHUNKS
    f32, bf16 = jnp.float32, jnp.bfloat16

    def lanes(at, size):
        return pl.ds(pl.multiple_of(at * size, size), size)

    mine = lanes(c, wide)
    weights = ((w_kv, all_kv), (w_o, all_o), (w_q, all_q))

    barrier = pltpu.get_barrier_semaphore()

    def greet(where):
        pl.semaphore_signal(
            barrier, inc=1, device_id=where, device_id_type=pl.DeviceIdType.MESH
        )

    @pl.when(s > 0)
    def _():
        greet((g, s - 1, c))

    @pl.when(s < n - 1)
    def _():
        greet((g, s + 1, c))

    for d in range(1, groups):
        greet(((g + d) % groups, s, c))
    for d in range(1, sections):
        greet((g, s, (c + d) % sections))

    beside = (s + n - 1) // n + (2 * n - 2 - s) // n
    pl.semaphore_wait(barrier, beside + groups + sections - 2)

    def remote(src, dst, send, recv, where):
        return pltpu.make_async_remote_copy(
            src_ref=src,
            dst_ref=dst,
            send_sem=send,
            recv_sem=recv,
            device_id=where,
            device_id_type=pl.DeviceIdType.MESH,
        )

    def spot(item, shard, part):
        w, chunk = item
        src, dst = weights[w]
        half = src.shape[0] // groups
        rows = pl.ds(pl.multiple_of((shard * groups + part) * half, half), half)
        return dst.at[rows, :] if chunk is None else dst.at[rows, lanes(chunk, span)]

    def source(item):
        w, chunk = item
        src, _ = weights[w]
        half = src.shape[0] // groups
        rows = lanes(g, half)
        return src.at[rows, :] if chunk is None else src.at[rows, lanes(chunk, span)]

    def index(item):
        w, chunk = item
        return w if chunk is None else w + chunk

    def up(item, shard, own=False):
        i, there = index(item), spot(item, shard, g)
        src = source(item) if own else there
        return remote(src, there, up_sem.at[i, shard], zrecv.at[i, shard], (g, s + 1, c))

    def down(item, shard, own=False):
        i, there = index(item), spot(item, shard, g)
        src = source(item) if own else there
        return remote(src, there, down_sem.at[i, shard], zrecv.at[i, shard], (g, s - 1, c))

    def across(item, shard, d, part):
        i, there = index(item), spot(item, shard, part)
        return remote(
            there, there, ysend.at[i, shard, d], yrecv.at[i, shard, d], ((g + d) % groups, s, c)
        )

    def write_up(shard, own=False):
        there = all_writes.at[shard, :, mine]
        return remote(
            writes if own else there, there, wsend.at[shard], wrecv.at[shard], (g, s + 1, c)
        )

    def write_peer(shard, d, origin):
        there = all_writes.at[shard, :, lanes(origin, wide)]
        return remote(
            there, there, psend.at[shard, d], precv.at[shard, d], (g, s, (c + d) % sections)
        )

    def own_copy(w):
        src, dst = weights[w]
        return pltpu.make_async_copy(src, dst.at[lanes(s, src.shape[0]), :], local.at[w])

    def start_own(item):
        @pl.when(s < n - 1)
        def _():
            up(item, s, True).start()

        @pl.when(s > 0)
        def _():
            down(item, s, True).start()

    def service(item):
        @pl.loop(1, n)
        def _(k):
            @pl.when(s - k >= 0)
            def _():
                up(item, s - k).wait_recv()

                @pl.when(s < n - 1)
                def _():
                    up(item, s - k).start()

                for d in range(1, groups):
                    across(item, s - k, d, g).start()

            @pl.when(s + k < n)
            def _():
                down(item, s + k).wait_recv()

                @pl.when(s > 0)
                def _():
                    down(item, s + k).start()

                for d in range(1, groups):
                    across(item, s + k, d, g).start()

    def finish(item):
        @pl.loop(0, n)
        def _(shard):
            @pl.when(shard != s)
            def _():
                for d in range(1, groups):
                    across(item, shard, d, (g + groups - d) % groups).wait_recv()

    def drain(item):
        @pl.loop(0, n)
        def _(shard):
            @pl.when(shard != s)
            def _():
                for d in range(1, groups):
                    across(item, shard, d, g).wait_send()

            @pl.when((shard <= s) & (s < n - 1))
            def _():
                up(item, shard).wait_send()

            @pl.when((shard >= s) & (s > 0))
            def _():
                down(item, shard).wait_send()

    kv_item, o_item = (0, None), (1, None)

    def q_item(chunk):
        return (2, chunk)

    @pl.when(s < n - 1)
    def _():
        write_up(s, True).start()

    start_own(kv_item)
    start_own(o_item)
    for w in range(3):
        own_copy(w).start()

    strip = 32

    def norm_rows(from_ref, to_row):
        @pl.loop(0, from_ref.shape[0] // strip)
        def _(r):
            x = from_ref[lanes(r, strip), :].astype(f32)
            scale = lax.rsqrt(jnp.mean(x * x, axis=-1, keepdims=True) + epsilon)
            to = pl.ds(pl.multiple_of(to_row + r * strip, strip), strip)
            normed[to, :] = (x * scale * gain[...]).astype(bf16)
            scales[to, :] = scale

    norm_rows(rows_in, MEM)

    whole_gate = gate[...]
    high = whole_gate.astype(bf16)
    rest = whole_gate - high.astype(f32)
    middle = rest.astype(bf16)
    gates[0] = high
    gates[1] = middle
    gates[2] = (rest - middle.astype(f32)).astype(bf16)

    keyed = lax.broadcasted_iota(jnp.int32, (BLK, BLK), 0)
    asked = lax.broadcasted_iota(jnp.int32, (BLK, BLK), 1)
    blocks = count // BLK
    for b in range(blocks):
        to = slice(b * BLK, (b + 1) * BLK)
        seen = jnp.where(pattern[b, 0] > 0, 0.0, masked_score)
        bias[:MEM, to] = jnp.full((MEM, BLK), seen, f32)
        for e in range(blocks):
            where = slice(MEM + e * BLK, MEM + (e + 1) * BLK)
            if e == b:
                bias[where, to] = jnp.where(keyed <= asked, 0.0, masked_score).astype(f32)
            elif e < b:
                seen = jnp.where(pattern[b, 1 + e] > 0, 0.0, masked_score)
                bias[where, to] = jnp.full((BLK, BLK), seen, f32)
            else:
                bias[where, to] = jnp.full((BLK, BLK), masked_score, f32)

    @pl.loop(1, n)
    def _(k):
        @pl.when(s - k >= 0)
        def _():
            write_up(s - k).wait_recv()

            @pl.when(s < n - 1)
            def _():
                write_up(s - k).start()

            for d in range(1, sections):
                write_peer(s - k, d, c).start()

    service(kv_item)
    start_own(q_item(0))
    start_own(q_item(1))

    state[...] = jnp.zeros_like(state)
    cut = width // HEADS

    @pl.loop(0, n)
    def _(k):
        @pl.when(k < s)
        def _():
            for d in range(1, sections):
                write_peer(k, d, (c + sections - d) % sections).wait_recv()
            w = all_writes[k]
            logits = sum(jnp.dot(w, gates[p], preferred_element_type=f32) for p in range(3))
            keep = jax.nn.sigmoid(logits + gate_bias[...])
            for h in range(HEADS):
                at = slice(h * cut, (h + 1) * cut)
                share = keep[:, h : h + 1]
                state[:, at] = share * state[:, at] + (1.0 - share) * w[:, at].astype(f32)

    memory[...] = state[...].astype(bf16)
    norm_rows(memory, 0)

    service(o_item)
    start_own(q_item(2))
    start_own(q_item(3))

    own_copy(0).wait()
    finish(kv_item)
    for kind, to in ((0, keys), (1, values)):
        part = jnp.dot(
            normed[...], all_kv[:, kind * span : (kind + 1) * span], preferred_element_type=f32
        ).astype(bf16)
        for h in range(KV_HEADS):
            to[h] = part[:, h * HEAD : (h + 1) * HEAD]

    service(q_item(0))

    own_copy(1).wait()
    finish(o_item)

    @pl.loop(0, KV_HEADS)
    def _(j):
        dmixed[j] = lax.dot_general(
            upstream[...], all_o[lanes(j, span), :], NT, preferred_element_type=f32
        ).astype(bf16)

    own_copy(2).wait()

    @pl.loop(0, KV_HEADS)
    def _(j):
        @pl.when(j < KV_HEADS - 1)
        def _():
            service(q_item(j + 1))

        finish(q_item(j))
        queries = jnp.dot(
            normed[MEM:, :], all_q[:, lanes(j, span)], preferred_element_type=f32
        ).astype(bf16)
        key, value = keys[j], values[j]
        pulled = dmixed[j]
        dkey = jnp.zeros(key.shape, f32)
        dvalue = jnp.zeros(value.shape, f32)
        dquery = []
        for h in range(GROUP):
            at = slice(h * HEAD, (h + 1) * HEAD)
            query, dhead = queries[:, at], pulled[:, at]
            scores = lax.dot_general(key, query, NT, preferred_element_type=f32)
            scores = scores * HEAD ** (-0.5) + bias[...]
            raised = jnp.exp(scores - jnp.max(scores, axis=0, keepdims=True))
            probs = raised * (1.0 / jnp.sum(raised, axis=0, keepdims=True))
            dprobs = lax.dot_general(value, dhead, NT, preferred_element_type=f32)
            dprobs = dprobs.astype(bf16).astype(f32)
            drop = jnp.sum(probs * dprobs, axis=0, keepdims=True)
            dscores = (probs * (dprobs - drop) * HEAD ** (-0.5)).astype(bf16)
            dvalue += jnp.dot(probs.astype(bf16), dhead, preferred_element_type=f32)
            dkey += jnp.dot(dscores, query, preferred_element_type=f32)
            dquery.append(lax.dot_general(key, dscores, TN, preferred_element_type=f32))
        dkeys[j] = dkey.astype(bf16)
        dvalues[j] = dvalue.astype(bf16)
        dq[:, lanes(j, span)] = jnp.concatenate(dquery, axis=0).T.astype(bf16)

    dkv = jnp.concatenate(
        [dkeys[h] for h in range(KV_HEADS)] + [dvalues[h] for h in range(KV_HEADS)], axis=1
    )
    tile = 256

    @pl.loop(0, width // tile)
    def _(t):
        at = lanes(t, tile)
        both = lax.dot_general(dkv, all_kv[at, :], NT, preferred_element_type=f32).astype(bf16)
        ones = lax.dot_general(dq[...], all_q[at, :], NT, preferred_element_type=f32).astype(bf16)
        dnormed[:MEM, at] = both[:MEM]
        dnormed[MEM:, at] = (both[MEM:].astype(f32) + ones.astype(f32)).astype(bf16)

    def pull_rows(from_ref, to_ref, from_row, extra):
        @pl.loop(0, from_ref.shape[0] // strip)
        def _(r):
            here = lanes(r, strip)
            there = pl.ds(pl.multiple_of(from_row + r * strip, strip), strip)
            x = from_ref[here, :].astype(f32)
            scale = scales[there, :]
            grown = dnormed[there, :].astype(f32) * gain[...]
            total = jnp.sum(grown * x, axis=-1, keepdims=True)
            dx = grown * scale - x * (total * scale * scale * scale * (1.0 / width))
            if extra is not None:
                dx = dx.astype(bf16).astype(f32) + extra[here, :].astype(f32)
            to_ref[here, :] = dx.astype(bf16)

    pull_rows(memory, grad_memory, 0, None)
    pull_rows(rows_in, grad_rows, MEM, upstream)

    @pl.loop(0, n)
    def _(shard):
        @pl.when(shard < s)
        def _():
            for d in range(1, sections):
                write_peer(shard, d, c).wait_send()

        @pl.when((shard <= s) & (s < n - 1))
        def _():
            write_up(shard).wait_send()

    drain(kv_item)
    drain(o_item)

    @pl.loop(0, CHUNKS)
    def _(j):
        drain(q_item(j))


def per_device(
    n,
    groups,
    sections,
    writes,
    layer_inputs,
    upstream,
    pattern,
    w_q,
    w_kv,
    w_o,
    norm_gain,
    gate_weight,
    gate_bias,
):
    count, width = layer_inputs.shape[2:]
    total = MEM + count
    span = HEADS * HEAD // CHUNKS
    anywhere = pl.BlockSpec(memory_space=pl.ANY)
    near = pl.BlockSpec(memory_space=pltpu.VMEM)
    dma = pltpu.SemaphoreType.DMA
    bf16, f32 = jnp.bfloat16, jnp.float32
    items = 2 + CHUNKS
    grads = pl.pallas_call(
        functools.partial(layer_kernel, n, groups, sections),
        out_shape=[
            jax.ShapeDtypeStruct((count, width), bf16),
            jax.ShapeDtypeStruct((MEM, width), bf16),
        ],
        in_specs=[pl.BlockSpec(memory_space=pltpu.SMEM), anywhere, near, near, near, near, near]
        + [anywhere] * 3,
        out_specs=[near, near],
        scratch_shapes=[
            pltpu.VMEM((n, MEM, width), bf16),
            pltpu.VMEM((width, w_kv.shape[2]), bf16),
            pltpu.VMEM((width, HEADS * HEAD), bf16),
            pltpu.VMEM((HEADS * HEAD, width), bf16),
            pltpu.VMEM((total, width), bf16),
            pltpu.VMEM((total, 1), f32),
            pltpu.VMEM((MEM, width), bf16),
            pltpu.VMEM((MEM, width), f32),
            pltpu.VMEM((3, width, HEADS), bf16),
            pltpu.VMEM((KV_HEADS, total, HEAD), bf16),
            pltpu.VMEM((KV_HEADS, total, HEAD), bf16),
            pltpu.VMEM((total, count), f32),
            pltpu.VMEM((KV_HEADS, count, span), bf16),
            pltpu.VMEM((count, HEADS * HEAD), bf16),
            pltpu.VMEM((KV_HEADS, total, HEAD), bf16),
            pltpu.VMEM((KV_HEADS, total, HEAD), bf16),
            pltpu.VMEM((total, width), bf16),
            dma((items, n)),
            dma((items, n)),
            dma((items, n)),
            dma((items, n, groups)),
            dma((items, n, groups)),
            dma((n,)),
            dma((n,)),
            dma((n, sections)),
            dma((n, sections)),
            dma((3,)),
        ],
        compiler_params=pltpu.CompilerParams(
            collective_id=0, has_side_effects=True, vmem_limit_bytes=56 * 1024 * 1024
        ),
    )(
        pattern[0],
        writes[0],
        layer_inputs[0, 0],
        upstream[0, 0],
        norm_gain,
        gate_weight[0],
        gate_bias,
        w_kv[0],
        w_q[0],
        w_o[0],
    )
    return (grads[0][None, None], grads[1][None, None])


def solution(mesh):
    placed = (
        P(("groups", "seg"), None, "section"),
        P("section", ("groups", "seg"), None, None),
        P("section", ("groups", "seg"), None, None),
        P(("groups", "seg"), None, None),
        P("section", "seg", None),
        P("section", "seg", None),
        P("section", "seg", None),
        P("section", None),
        P("section", None, None),
        P("section", None),
    )
    sizes = (mesh.shape["seg"], mesh.shape["groups"], mesh.shape["section"])
    return jax.shard_map(
        functools.partial(per_device, *sizes),
        mesh=mesh,
        in_specs=placed,
        out_specs=(
            P("section", ("groups", "seg"), None, None),
            P("section", ("groups", "seg"), None, None),
        ),
        check_vma=False,
    )
```

time: 330 us -> 136 us (0.41); the launches traced: 325 us -> 136 us
  waiting for transfers between devices: 247 us -> 0 us
  Pallas kernels: 0 us -> 130 us
  matrix products: 21.7 us -> 0 us
  blocking collectives: 20.6 us -> 0 us
  other arithmetic: 14.6 us -> 0 us
  between operations: 14.1 us -> 0.65 us
    all_gather x4 -> x0, waiting for transfers between devices: 245 us -> none  [the longest x1 77.1 us: carried_in(): gathered = jax.tree.map(lambda a: lax.all_gather(a, axis), part)]
    pallas_call x0 -> x1, Pallas kernels: none -> 130 us  [per_device(): pl.pallas_call(functools.partial(layer_kernel, n, groups, sections), out_...]
    dot_general x11 -> x0, matrix products: 21.7 us -> none  [the longest x2 5.53 us: apply_layer(): jnp.dot(normed[memory_rows:], query_weight, preferred_element_type=jnp.fl...]
    all_gather x2 -> x0, blocking collectives: 20.6 us -> none  [the longest x1 13.2 us: carried_in(): gathered = jax.tree.map(lambda a: lax.all_gather(a, axis), part)]
    add x3 -> x0, other arithmetic: 6.42 us -> none  [compose(): return (former[0] * latter[0], carried.reshape(MEM, width) + latter[1])]
    unnamed x20 -> x5, local copies, waits for them, and re-layouts: 0.98 us -> 5.37 us
    mul x2 -> x0, other arithmetic: 3.66 us -> none  [the longest x1 2.58 us: attend_rows(): jnp.einsum('qgre,sge->grqs', grouped, keys, preferred_element_type=jnp.fl...]
  transfers between devices with their start and end apart: 4 -> 0, of which waited for: 4 -> 0; matrix products, arithmetic and copies ran while one was open for 7% -> 0% of each run, Pallas kernels for 0% -> 0%
where the time goes in v2:
time: 136 us
  Pallas kernels  130 us (96%)
  local copies, waits for them, and re-layouts  5.37 us (4%)
    pallas_call x1, Pallas kernels, per_device(): pl.pallas_call(functools.partial(layer_kernel, n, groups, sections), out_...  130 us
    unnamed x5, local copies, waits for them, and re-layouts  5.37 us

profile of v2, /device:TPU:24, one launch (start us, length us, event | category | flops | bytes accessed | tf_op | source)
XLA Modules:
  0.0 136.3 jit_solution(12241090650660897311)
XLA Ops:
  0.6 2.2 %copy.12 = f32[1,2048,16]{2,1,0:T(8,128)} copy(f32[1,2048,16]{1,2,0:T(8,128)} %param.18) | data formatting | bytes 262144 | tf_op args[8]
  2.8 130.3 %shard_map.113 = (bf16[256,2048]{1,0:T(8,128)(2,1)}, bf16[128,2048]{1,0:T(8,128)(2,1)}) custom-call(s32[2,3]{1,0:T(2,128)} %bitcast.19, bf16[128,512]{1,0:T(8,128)(2,1)} %bitcast.18, bf16[256,2048]{1,0:T(8,128)(2,1)} %bitcast.11, bf16[256,2048]{1,0:T(8,128)(2,1)} %bitcast.12, f32[1,2048]{1,0:T(1,128)} %gain.1, f32[2048,16]{1,0:T(8,128)} %bitcast.10, ...), custom_call_target="tpu_custom_call" | custom-call | tf_op jit(solution)/shard_map/pallas_call | solution.py:436
  133.2 0.0 copy-start
  133.2 2.4 %copy.15 = bf16[1,1,256,2048]{3,2,1,0:T(8,128)(2,1)} copy(bf16[1,1,256,2048]{3,2,1,0:T(8,128)(2,1)} %bitcast.15) | data formatting | bytes 2097152
  135.5 0.0 copy-done
  135.5 0.8 copy.16
Async XLA Ops:
  133.2 2.4 %copy-start = (bf16[128,2048]{1,0:T(8,128)(2,1)S(1)}, bf16[128,2048]{1,0:T(8,128)(2,1)}, u32[]{:S(2)}) copy-start(bf16[128,2048]{1,0:T(8,128)(2,1)} %get-tuple-element.5) | copy-start | bytes 1572868

commit v3 on v2

--- a/solution.py
+++ b/solution.py
@@ -20,6 +20,8 @@
 NT = (((1,), (1,)), ((), ()))
 TN = (((0,), (0,)), ((), ()))
 CHUNKS = KV_HEADS
+PAIR = 2
+OUTS = 2
 
 
 def layer_kernel(
@@ -57,7 +59,8 @@
     dnormed,
     *sems,
 ):
-    up_sem, down_sem, zrecv, ysend, yrecv, wsend, wrecv, psend, precv, local = sems
+    up_sem, down_sem, far_up_sem, far_down_sem, zrecv, ysend, yrecv = sems[:7]
+    wsend, wrecv, psend, precv, local = sems[7:]
     g = lax.axis_index("groups")
     s = lax.axis_index("seg")
     c = lax.axis_index("section")
@@ -87,12 +90,20 @@
     def _():
         greet((g, s + 1, c))
 
+    @pl.when(s > 1)
+    def _():
+        greet((g, s - 2, c))
+
+    @pl.when(s < n - 2)
+    def _():
+        greet((g, s + 2, c))
+
     for d in range(1, groups):
         greet(((g + d) % groups, s, c))
     for d in range(1, sections):
         greet((g, s, (c + d) % sections))
 
-    beside = (s + n - 1) // n + (2 * n - 2 - s) // n
+    beside = (s + n - 1) // n + (2 * n - 2 - s) // n + (s + n - 2) // n + (2 * n - 3 - s) // n
     pl.semaphore_wait(barrier, beside + groups + sections - 2)
 
     def remote(src, dst, send, recv, where):
@@ -105,33 +116,39 @@
             device_id_type=pl.DeviceIdType.MESH,
         )
 
+    bases = (0, PAIR, PAIR + OUTS)
+    widths = (all_kv.shape[1] // PAIR, width // OUTS, span)
+
     def spot(item, shard, part):
         w, chunk = item
-        src, dst = weights[w]
-        half = src.shape[0] // groups
+        half = weights[w][0].shape[0] // groups
         rows = pl.ds(pl.multiple_of((shard * groups + part) * half, half), half)
-        return dst.at[rows, :] if chunk is None else dst.at[rows, lanes(chunk, span)]
+        return weights[w][1].at[rows, lanes(chunk, widths[w])]
 
     def source(item):
         w, chunk = item
-        src, _ = weights[w]
-        half = src.shape[0] // groups
-        rows = lanes(g, half)
-        return src.at[rows, :] if chunk is None else src.at[rows, lanes(chunk, span)]
+        src = weights[w][0]
+        return src.at[lanes(g, src.shape[0] // groups), lanes(chunk, widths[w])]
 
     def index(item):
-        w, chunk = item
-        return w if chunk is None else w + chunk
-
-    def up(item, shard, own=False):
+        return bases[item[0]] + item[1]
+
+    def along(item, shard, sems, step, own=False):
         i, there = index(item), spot(item, shard, g)
         src = source(item) if own else there
-        return remote(src, there, up_sem.at[i, shard], zrecv.at[i, shard], (g, s + 1, c))
+        return remote(src, there, sems.at[i, shard], zrecv.at[i, shard], (g, s + step, c))
+
+    def up(item, shard, own=False):
+        return along(item, shard, up_sem, 1, own)
 
     def down(item, shard, own=False):
-        i, there = index(item), spot(item, shard, g)
-        src = source(item) if own else there
-        return remote(src, there, down_sem.at[i, shard], zrecv.at[i, shard], (g, s - 1, c))
+        return along(item, shard, down_sem, -1, own)
+
+    def far_up(item):
+        return along(item, s, far_up_sem, 2, True)
+
+    def far_down(item):
+        return along(item, s, far_down_sem, -2, True)
 
     def across(item, shard, d, part):
         i, there = index(item), spot(item, shard, part)
@@ -156,6 +173,14 @@
         return pltpu.make_async_copy(src, dst.at[lanes(s, src.shape[0]), :], local.at[w])
 
     def start_own(item):
+        @pl.when(s < n - 2)
+        def _():
+            far_up(item).start()
+
+        @pl.when(s > 1)
+        def _():
+            far_down(item).start()
+
         @pl.when(s < n - 1)
         def _():
             up(item, s, True).start()
@@ -171,7 +196,7 @@
             def _():
                 up(item, s - k).wait_recv()
 
-                @pl.when(s < n - 1)
+                @pl.when((k > 1) & (s < n - 1))
                 def _():
                     up(item, s - k).start()
 
@@ -182,7 +207,7 @@
             def _():
                 down(item, s + k).wait_recv()
 
-                @pl.when(s > 0)
+                @pl.when((k > 1) & (s > 0))
                 def _():
                     down(item, s + k).start()
 
@@ -205,15 +230,27 @@
                 for d in range(1, groups):
                     across(item, shard, d, g).wait_send()
 
-            @pl.when((shard <= s) & (s < n - 1))
+            @pl.when((shard <= s) & (shard != s - 1) & (s < n - 1))
             def _():
                 up(item, shard).wait_send()
 
-            @pl.when((shard >= s) & (s > 0))
+            @pl.when((shard >= s) & (shard != s + 1) & (s > 0))
             def _():
                 down(item, shard).wait_send()
 
-    kv_item, o_item = (0, None), (1, None)
+        @pl.when(s < n - 2)
+        def _():
+            far_up(item).wait_send()
+
+        @pl.when(s > 1)
+        def _():
+            far_down(item).wait_send()
+
+    def kv_item(chunk):
+        return (0, chunk)
+
+    def o_item(chunk):
+        return (1, chunk)
 
     def q_item(chunk):
         return (2, chunk)
@@ -222,10 +259,8 @@
     def _():
         write_up(s, True).start()
 
-    start_own(kv_item)
-    start_own(o_item)
-    for w in range(3):
-        own_copy(w).start()
+    start_own(kv_item(0))
+    start_own(kv_item(1))
 
     strip = 32
 
@@ -239,6 +274,9 @@
             scales[to, :] = scale
 
     norm_rows(rows_in, MEM)
+    start_own(o_item(0))
+    for w in range(3):
+        own_copy(w).start()
 
     whole_gate = gate[...]
     high = whole_gate.astype(bf16)
@@ -278,9 +316,10 @@
             for d in range(1, sections):
                 write_peer(s - k, d, c).start()
 
-    service(kv_item)
+    service(kv_item(0))
+    start_own(o_item(1))
+    service(kv_item(1))
     start_own(q_item(0))
-    start_own(q_item(1))
 
     state[...] = jnp.zeros_like(state)
     cut = width // HEADS
@@ -292,7 +331,9 @@
             for d in range(1, sections):
                 write_peer(k, d, (c + sections - d) % sections).wait_recv()
             w = all_writes[k]
-            logits = sum(jnp.dot(w, gates[p], preferred_element_type=f32) for p in range(3))
+            logits = sum(
+                lax.dot_general(w, gates[p], NT, preferred_element_type=f32) for p in range(3)
+            )
             keep = jax.nn.sigmoid(logits + gate_bias[...])
             for h in range(HEADS):
                 at = slice(h * cut, (h + 1) * cut)
@@ -302,12 +343,12 @@
     memory[...] = state[...].astype(bf16)
     norm_rows(memory, 0)
 
-    service(o_item)
-    start_own(q_item(2))
-    start_own(q_item(3))
+    service(o_item(0))
+    start_own(q_item(1))
 
     own_copy(0).wait()
-    finish(kv_item)
+    finish(kv_item(0))
+    finish(kv_item(1))
     for kind, to in ((0, keys), (1, values)):
         part = jnp.dot(
             normed[...], all_kv[:, kind * span : (kind + 1) * span], preferred_element_type=f32
@@ -315,10 +356,14 @@
         for h in range(KV_HEADS):
             to[h] = part[:, h * HEAD : (h + 1) * HEAD]
 
+    service(o_item(1))
+    start_own(q_item(2))
+    start_own(q_item(3))
     service(q_item(0))
 
     own_copy(1).wait()
-    finish(o_item)
+    finish(o_item(0))
+    finish(o_item(1))
 
     @pl.loop(0, KV_HEADS)
     def _(j):
@@ -402,8 +447,13 @@
         def _():
             write_up(shard).wait_send()
 
-    drain(kv_item)
-    drain(o_item)
+    @pl.loop(0, PAIR)
+    def _(j):
+        drain(kv_item(j))
+
+    @pl.loop(0, OUTS)
+    def _(j):
+        drain(o_item(j))
 
     @pl.loop(0, CHUNKS)
     def _(j):
@@ -432,7 +482,7 @@
     near = pl.BlockSpec(memory_space=pltpu.VMEM)
     dma = pltpu.SemaphoreType.DMA
     bf16, f32 = jnp.bfloat16, jnp.float32
-    items = 2 + CHUNKS
+    items = PAIR + OUTS + CHUNKS
     grads = pl.pallas_call(
         functools.partial(layer_kernel, n, groups, sections),
         out_shape=[
@@ -451,7 +501,7 @@
             pltpu.VMEM((total, 1), f32),
             pltpu.VMEM((MEM, width), bf16),
             pltpu.VMEM((MEM, width), f32),
-            pltpu.VMEM((3, width, HEADS), bf16),
+            pltpu.VMEM((3, HEADS, width), bf16),
             pltpu.VMEM((KV_HEADS, total, HEAD), bf16),
             pltpu.VMEM((KV_HEADS, total, HEAD), bf16),
             pltpu.VMEM((total, count), f32),
@@ -460,6 +510,8 @@
             pltpu.VMEM((KV_HEADS, total, HEAD), bf16),
             pltpu.VMEM((KV_HEADS, total, HEAD), bf16),
             pltpu.VMEM((total, width), bf16),
+            dma((items, n)),
+            dma((items, n)),
             dma((items, n)),
             dma((items, n)),
             dma((items, n)),
@@ -480,7 +532,7 @@
         layer_inputs[0, 0],
         upstream[0, 0],
         norm_gain,
-        gate_weight[0],
+        gate_weight[0].T,
         gate_bias,
         w_kv[0],
         w_q[0],

time: 136 us -> 174 us (1.28)
  Pallas kernels: 130 us -> 170 us
  local copies, waits for them, and re-layouts: 5.37 us -> 3.16 us
    pallas_call x1, Pallas kernels: 130 us -> 170 us  [per_device(): pl.pallas_call(functools.partial(layer_kernel, n, groups, sections), out_...]
    unnamed x5 -> x4, local copies, waits for them, and re-layouts: 5.37 us -> 3.16 us
where the time goes in v3:
time: 174 us
  Pallas kernels  170 us (98%)
  local copies, waits for them, and re-layouts  3.16 us (2%)
    pallas_call x1, Pallas kernels, per_device(): pl.pallas_call(functools.partial(layer_kernel, n, groups, sections), out_...  170 us

profile of v3, /device:TPU:24, one launch (start us, length us, event | category | flops | bytes accessed | tf_op | source)
XLA Modules:
  0.0 174.0 jit_solution(5699916967771486860)
XLA Ops:
  0.6 170.2 %shard_map.113 = (bf16[256,2048]{1,0:T(8,128)(2,1)}, bf16[128,2048]{1,0:T(8,128)(2,1)}) custom-call(s32[2,3]{1,0:T(2,128)} %bitcast.21, bf16[128,512]{1,0:T(8,128)(2,1)} %bitcast.19, bf16[256,2048]{1,0:T(8,128)(2,1)} %bitcast.13, bf16[256,2048]{1,0:T(8,128)(2,1)} %bitcast.14, f32[1,2048]{1,0:T(1,128)} %gain.1, f32[16,2048]{1,0:T(8,128)} %bitcast.20, ...), custom_call_target="tpu_custom_call" | custom-call | tf_op jit(solution)/shard_map/pallas_call | solution.py:486
  170.8 0.0 copy-start
  170.9 2.4 %copy.14 = bf16[1,1,256,2048]{3,2,1,0:T(8,128)(2,1)} copy(bf16[1,1,256,2048]{3,2,1,0:T(8,128)(2,1)} %bitcast.12) | data formatting | bytes 2097152
  173.2 0.0 copy-done
  173.2 0.8 copy.15
Async XLA Ops:
  170.8 2.4 %copy-start = (bf16[128,2048]{1,0:T(8,128)(2,1)S(1)}, bf16[128,2048]{1,0:T(8,128)(2,1)}, u32[]{:S(2)}) copy-start(bf16[128,2048]{1,0:T(8,128)(2,1)} %get-tuple-element.5) | copy-start | bytes 1572868

commit v4 on v2

--- a/solution.py
+++ b/solution.py
@@ -223,9 +223,6 @@
         write_up(s, True).start()
 
     start_own(kv_item)
-    start_own(o_item)
-    for w in range(3):
-        own_copy(w).start()
 
     strip = 32
 
@@ -239,6 +236,9 @@
             scales[to, :] = scale
 
     norm_rows(rows_in, MEM)
+    start_own(o_item)
+    for w in range(3):
+        own_copy(w).start()
 
     whole_gate = gate[...]
     high = whole_gate.astype(bf16)
@@ -292,7 +292,9 @@
             for d in range(1, sections):
                 write_peer(k, d, (c + sections - d) % sections).wait_recv()
             w = all_writes[k]
-            logits = sum(jnp.dot(w, gates[p], preferred_element_type=f32) for p in range(3))
+            logits = sum(
+                lax.dot_general(w, gates[p], NT, preferred_element_type=f32) for p in range(3)
+            )
             keep = jax.nn.sigmoid(logits + gate_bias[...])
             for h in range(HEADS):
                 at = slice(h * cut, (h + 1) * cut)
@@ -374,7 +376,7 @@
         dnormed[:MEM, at] = both[:MEM]
         dnormed[MEM:, at] = (both[MEM:].astype(f32) + ones.astype(f32)).astype(bf16)
 
-    def pull_rows(from_ref, to_ref, from_row, extra):
+    def pull_rows(from_ref, to_ref, from_row):
         @pl.loop(0, from_ref.shape[0] // strip)
         def _(r):
             here = lanes(r, strip)
@@ -384,12 +386,10 @@
             grown = dnormed[there, :].astype(f32) * gain[...]
             total = jnp.sum(grown * x, axis=-1, keepdims=True)
             dx = grown * scale - x * (total * scale * scale * scale * (1.0 / width))
-            if extra is not None:
-                dx = dx.astype(bf16).astype(f32) + extra[here, :].astype(f32)
             to_ref[here, :] = dx.astype(bf16)
 
-    pull_rows(memory, grad_memory, 0, None)
-    pull_rows(rows_in, grad_rows, MEM, upstream)
+    pull_rows(memory, grad_memory, 0)
+    pull_rows(rows_in, grad_rows, MEM)
 
     @pl.loop(0, n)
     def _(shard):
@@ -451,7 +451,7 @@
             pltpu.VMEM((total, 1), f32),
             pltpu.VMEM((MEM, width), bf16),
             pltpu.VMEM((MEM, width), f32),
-            pltpu.VMEM((3, width, HEADS), bf16),
+            pltpu.VMEM((3, HEADS, width), bf16),
             pltpu.VMEM((KV_HEADS, total, HEAD), bf16),
             pltpu.VMEM((KV_HEADS, total, HEAD), bf16),
             pltpu.VMEM((total, count), f32),
@@ -480,13 +480,14 @@
         layer_inputs[0, 0],
         upstream[0, 0],
         norm_gain,
-        gate_weight[0],
+        gate_weight[0].T,
         gate_bias,
         w_kv[0],
         w_q[0],
         w_o[0],
     )
-    return (grads[0][None, None], grads[1][None, None])
+    grad_rows = (grads[0].astype(f32) + upstream[0, 0].astype(f32)).astype(bf16)
+    return (grad_rows[None, None], grads[1][None, None])
 
 
 def solution(mesh):

time: 136 us -> 134 us (0.985)
  local copies, waits for them, and re-layouts: 5.37 us -> 0.8 us
  other arithmetic: 0 us -> 2.65 us
    unnamed x5, local copies, waits for them, and re-layouts: 5.37 us -> 0.8 us
    broadcast_in_dim x0 -> x1, other arithmetic: none -> 2.65 us  [per_device(): return (grad_rows[None, None], grads[1][None, None])]
where the time goes in v4:
time: 134 us
  Pallas kernels  130 us (97%)
  other arithmetic  2.65 us (2%)
    pallas_call x1, Pallas kernels, per_device(): pl.pallas_call(functools.partial(layer_kernel, n, groups, sections), out_...  130 us

profile of v4, /device:TPU:24, one launch (start us, length us, event | category | flops | bytes accessed | tf_op | source)
XLA Modules:
  0.0 134.0 jit_solution(15523260482167591626)
XLA Ops:
  0.6 0.0 copy-start
  0.6 129.9 %shard_map.113 = (bf16[256,2048]{1,0:T(8,128)(2,1)}, bf16[128,2048]{1,0:T(8,128)(2,1)}) custom-call(s32[2,3]{1,0:T(2,128)} %bitcast.22, bf16[128,512]{1,0:T(8,128)(2,1)} %bitcast.20, bf16[256,2048]{1,0:T(8,128)(2,1)} %bitcast.15, bf16[256,2048]{1,0:T(8,128)(2,1)} %bitcast.14, f32[1,2048]{1,0:T(1,128)} %gain.1, f32[16,2048]{1,0:T(8,128)} %bitcast.21, ...), custom_call_target="tpu_custom_call" | custom-call | tf_op jit(solution)/shard_map/pallas_call | solution.py:436
  130.6 0.0 copy-done
  130.6 0.0 copy-start.1
  130.6 2.6 %fusion = bf16[1,1,256,2048]{3,2,1,0:T(8,128)(2,1)} fusion(bf16[256,2048]{1,0:T(8,128)(2,1)} %get-tuple-element.4, bf16[1,1,256,2048]{3,2,1,0:T(8,128)(2,1)S(1)} %copy-done), kind=kLoop, calls=%fused_computation.1 | loop fusion | flops 2097152 | bytes 3145728 | tf_op jit(solution)/shard_map/broadcast_in_dim | solution.py:490
  133.2 0.0 copy-done.1
  133.3 0.8 copy.13
Async XLA Ops:
  0.6 130.0 %copy-start = (bf16[1,1,256,2048]{3,2,1,0:T(8,128)(2,1)S(1)}, bf16[1,1,256,2048]{3,2,1,0:T(8,128)(2,1)}, u32[]{:S(2)}) copy-start(bf16[1,1,256,2048]{3,2,1,0:T(8,128)(2,1)} %param.12) | copy-start | bytes 3145732
  130.6 2.7 %copy-start.1 = (bf16[128,2048]{1,0:T(8,128)(2,1)S(1)}, bf16[128,2048]{1,0:T(8,128)(2,1)}, u32[]{:S(2)}) copy-start(bf16[128,2048]{1,0:T(8,128)(2,1)} %get-tuple-element.5) | copy-start | bytes 1572868

commit v5 on v4

--- a/solution.py
+++ b/solution.py
@@ -55,6 +55,9 @@
     dkeys,
     dvalues,
     dnormed,
+    asking,
+    dasking,
+    dsums,
     *sems,
 ):
     up_sem, down_sem, zrecv, ysend, yrecv, wsend, wrecv, psend, precv, local = sems
@@ -164,8 +167,11 @@
         def _():
             down(item, s, True).start()
 
-    def service(item):
-        @pl.loop(1, n)
+    def service(item, first=1, last=n):
+        if first >= last:
+            return
+
+        @pl.loop(first, last)
         def _(k):
             @pl.when(s - k >= 0)
             def _():
@@ -318,6 +324,7 @@
             to[h] = part[:, h * HEAD : (h + 1) * HEAD]
 
     service(q_item(0))
+    service(q_item(1))
 
     own_copy(1).wait()
     finish(o_item)
@@ -332,22 +339,15 @@
 
     @pl.loop(0, KV_HEADS)
     def _(j):
-        @pl.when(j < KV_HEADS - 1)
-        def _():
-            service(q_item(j + 1))
-
         finish(q_item(j))
-        queries = jnp.dot(
+        asking[...] = jnp.dot(
             normed[MEM:, :], all_q[:, lanes(j, span)], preferred_element_type=f32
         ).astype(bf16)
-        key, value = keys[j], values[j]
-        pulled = dmixed[j]
-        dkey = jnp.zeros(key.shape, f32)
-        dvalue = jnp.zeros(value.shape, f32)
-        dquery = []
+        dsums[...] = jnp.zeros_like(dsums)
         for h in range(GROUP):
             at = slice(h * HEAD, (h + 1) * HEAD)
-            query, dhead = queries[:, at], pulled[:, at]
+            key, value = keys[j], values[j]
+            query, dhead = asking[:, at], dmixed[j][:, at]
             scores = lax.dot_general(key, query, NT, preferred_element_type=f32)
             scores = scores * HEAD ** (-0.5) + bias[...]
             raised = jnp.exp(scores - jnp.max(scores, axis=0, keepdims=True))
@@ -356,12 +356,19 @@
             dprobs = dprobs.astype(bf16).astype(f32)
             drop = jnp.sum(probs * dprobs, axis=0, keepdims=True)
             dscores = (probs * (dprobs - drop) * HEAD ** (-0.5)).astype(bf16)
-            dvalue += jnp.dot(probs.astype(bf16), dhead, preferred_element_type=f32)
-            dkey += jnp.dot(dscores, query, preferred_element_type=f32)
-            dquery.append(lax.dot_general(key, dscores, TN, preferred_element_type=f32))
-        dkeys[j] = dkey.astype(bf16)
-        dvalues[j] = dvalue.astype(bf16)
-        dq[:, lanes(j, span)] = jnp.concatenate(dquery, axis=0).T.astype(bf16)
+            dsums[0] += jnp.dot(dscores, query, preferred_element_type=f32)
+            dsums[1] += jnp.dot(probs.astype(bf16), dhead, preferred_element_type=f32)
+            dasking[at, :] = lax.dot_general(key, dscores, TN, preferred_element_type=f32)
+            first, last = 1 + h * (n - 1) // GROUP, 1 + (h + 1) * (n - 1) // GROUP
+            if first < last:
+
+                @pl.when(j < KV_HEADS - 2)
+                def _(first=first, last=last):
+                    service(q_item(j + 2), first, last)
+
+        dkeys[j] = dsums[0].astype(bf16)
+        dvalues[j] = dsums[1].astype(bf16)
+        dq[:, lanes(j, span)] = dasking[...].T.astype(bf16)
 
     dkv = jnp.concatenate(
         [dkeys[h] for h in range(KV_HEADS)] + [dvalues[h] for h in range(KV_HEADS)], axis=1
@@ -460,6 +467,9 @@
             pltpu.VMEM((KV_HEADS, total, HEAD), bf16),
             pltpu.VMEM((KV_HEADS, total, HEAD), bf16),
             pltpu.VMEM((total, width), bf16),
+            pltpu.VMEM((count, span), bf16),
+            pltpu.VMEM((span, count), f32),
+            pltpu.VMEM((2, total, HEAD), f32),
             dma((items, n)),
             dma((items, n)),
             dma((items, n)),

time: 134 us -> 135 us (level)
  no operation moved by 1% of the time
where the time goes in v5:
time: 135 us
  Pallas kernels  131 us (97%)
  other arithmetic  2.65 us (2%)
    pallas_call x1, Pallas kernels, per_device(): pl.pallas_call(functools.partial(layer_kernel, n, groups, sections), out_...  131 us

profile of v5, /device:TPU:24, one launch (start us, length us, event | category | flops | bytes accessed | tf_op | source)
XLA Modules:
  0.0 134.7 jit_solution(2947402021076442811)
XLA Ops:
  0.6 0.0 copy-start
  0.6 130.6 %shard_map.113 = (bf16[256,2048]{1,0:T(8,128)(2,1)}, bf16[128,2048]{1,0:T(8,128)(2,1)}) custom-call(s32[2,3]{1,0:T(2,128)} %bitcast.22, bf16[128,512]{1,0:T(8,128)(2,1)} %bitcast.20, bf16[256,2048]{1,0:T(8,128)(2,1)} %bitcast.15, bf16[256,2048]{1,0:T(8,128)(2,1)} %bitcast.14, f32[1,2048]{1,0:T(1,128)} %gain.1, f32[16,2048]{1,0:T(8,128)} %bitcast.21, ...), custom_call_target="tpu_custom_call" | custom-call | tf_op jit(solution)/shard_map/pallas_call | solution.py:443
  131.2 0.0 copy-done
  131.2 0.0 copy-start.1
  131.2 2.6 %fusion = bf16[1,1,256,2048]{3,2,1,0:T(8,128)(2,1)} fusion(bf16[256,2048]{1,0:T(8,128)(2,1)} %get-tuple-element.4, bf16[1,1,256,2048]{3,2,1,0:T(8,128)(2,1)S(1)} %copy-done), kind=kLoop, calls=%fused_computation.1 | loop fusion | flops 2097152 | bytes 3145728 | tf_op jit(solution)/shard_map/broadcast_in_dim | solution.py:500
  133.9 0.0 copy-done.1
  133.9 0.8 copy.13
Async XLA Ops:
  0.6 130.6 %copy-start = (bf16[1,1,256,2048]{3,2,1,0:T(8,128)(2,1)S(1)}, bf16[1,1,256,2048]{3,2,1,0:T(8,128)(2,1)}, u32[]{:S(2)}) copy-start(bf16[1,1,256,2048]{3,2,1,0:T(8,128)(2,1)} %param.12) | copy-start | bytes 3145732
  131.2 2.7 %copy-start.1 = (bf16[128,2048]{1,0:T(8,128)(2,1)S(1)}, bf16[128,2048]{1,0:T(8,128)(2,1)}, u32[]{:S(2)}) copy-start(bf16[128,2048]{1,0:T(8,128)(2,1)} %get-tuple-element.5) | copy-start | bytes 1572868
